TPU v7x, 32 devices: a whole 2x2x4 slice. The times are simulated.
32 devices in a mesh: expert: 8 (over y, x, core), dp: 4 (over z).
Axes of the slice: x: 2, y: 2, z: 4, core: 2. Of those that a mesh axis runs over, the one named last changes fastest.
Arguments:
- tokens: bfloat16 [4096, 2048], P(('expert', 'dp')), may hold values from -6 to 6
- expert_ids: int32 [4096, 8], P(('expert', 'dp')), may hold values from 0 to 15, all different within a row; in each aligned block of 128 rows (0 to 127, 128 to 255, ...) at most 72 rows name the same one
- router: bfloat16 [2048, 16], replicated, may hold values from -0.25 to 0.25
- w_gate: bfloat16 [16, 2048, 640], P('expert'), may hold values from -0.125 to 0.125
- w_up: bfloat16 [16, 2048, 640], P('expert'), may hold values from -0.125 to 0.125
- w_down: bfloat16 [16, 640, 2048], P('expert'), may hold values from -1 to 1
- out_grad: bfloat16 [4096, 2048], P(('expert', 'dp')), may hold values from -6 to 6
Outputs:
- mixed: bfloat16 [4096, 2048], P(('expert', 'dp'))
- token_grad: bfloat16 [4096, 2048], P(('expert', 'dp'))
- router_grad: float32 [2048, 16], replicated
- gate_grad: bfloat16 [16, 2048, 640], P('expert', 'dp')
- up_grad: bfloat16 [16, 2048, 640], P('expert', 'dp')
- down_grad: bfloat16 [16, 640, 2048], P('expert', None, 'dp')
Inputs may be any that keep to these rules, and one draw needn't show every extreme that they name: `expert_ids`: each row names 8 different experts; within the 128 rows of one device no expert is named more than 72 times.
All inputs are finite; a program needn't handle non-finite values.
Results may differ from a plain program's by a relative error of at most 0.008.
Values may be sent and summed in bfloat16 or wider, within the bound.
No kernel may reach another device: no remote copies, remote signals or barrier semaphores. Data moves between devices by JAX's collectives and lax.ppermute only.
A program may use at most 256 MiB of HBM per device.

v0:
```python
import jax
import jax.numpy as jnp
from jax import lax
from jax.sharding import PartitionSpec as P


def flat_rows(array):
    return array.reshape(array.shape[0], array.shape[1] * array.shape[2], array.shape[3])


def body(tokens, expert_ids, router, w_gate, w_up, w_down, out_grad):
    f32 = jnp.float32
    bf16 = jnp.bfloat16
    tok_dev, width = tokens.shape
    top = expert_ids.shape[1]
    n_experts = router.shape[1]
    local_experts = w_gate.shape[0]
    groups = lax.axis_size("expert")
    capacity = (tok_dev * top * 9 + 8 * n_experts - 1) // (8 * n_experts)
    n_assign = tok_dev * top
    flat_ids = expert_ids.reshape(-1)
    ladder = jnp.arange(n_experts, dtype=jnp.int32)
    onehot = (flat_ids[:, None] == ladder[None, :]).astype(jnp.int32)
    rank = jnp.sum((jnp.cumsum(onehot, axis=0) - onehot) * onehot, axis=1)
    owner = flat_ids // local_experts
    within = flat_ids % local_experts
    dest = (within * groups + owner) * capacity + rank
    slot_src = jnp.full((n_experts * capacity,), n_assign, jnp.int32)
    slot_src = slot_src.at[dest].set(jnp.arange(n_assign, dtype=jnp.int32))
    live = slot_src < n_assign
    slot_tok = jnp.where(live, slot_src // top, 0)
    logits = jnp.dot(tokens, router, preferred_element_type=f32)
    scores = jax.nn.sigmoid(logits)
    chosen = jnp.take_along_axis(scores, expert_ids, axis=1)
    total = jnp.sum(chosen, axis=1, keepdims=True)
    gates = chosen / total
    gate_slots = jnp.where(live, gates.reshape(-1)[jnp.minimum(slot_src, n_assign - 1)], 0.0)
    send = jnp.where(live[:, None], tokens[slot_tok], jnp.zeros((), bf16))
    send = send.reshape(local_experts, groups, capacity, width)
    piece = lax.all_to_all(send, "expert", split_axis=1, concat_axis=1, tiled=True)
    shape = piece.shape
    rows = flat_rows(piece)
    pre_gate = jnp.einsum("jrd,jdf->jrf", rows, w_gate, preferred_element_type=f32)
    pre_up = jnp.einsum("jrd,jdf->jrf", rows, w_up, preferred_element_type=f32)
    hidden = (pre_gate * jax.nn.sigmoid(pre_gate) * pre_up).astype(bf16)
    expert_out = jnp.einsum("jrf,jfd->jrd", hidden, w_down, preferred_element_type=f32).astype(bf16)
    hid_shape = (shape[0], shape[1], shape[2], hidden.shape[2])
    expert_out = expert_out.reshape(shape)
    hidden = hidden.reshape(hid_shape)
    results = (expert_out, hidden, piece, pre_gate.reshape(hid_shape), pre_up.reshape(hid_shape))
    expert_out = results[0]
    hidden = flat_rows(results[1])
    back = lax.all_to_all(expert_out, "expert", split_axis=1, concat_axis=1, tiled=True).reshape(
        n_experts * capacity, width
    )
    picked = back[dest].reshape(tok_dev, top, width)
    mixed = jnp.einsum("tk,tkd->td", gates, picked.astype(f32)).astype(bf16)
    gate_sens = jnp.einsum("tkd,td->tk", picked, out_grad, preferred_element_type=f32)
    grad_rows = (gate_slots[:, None] * out_grad[slot_tok].astype(f32)).astype(bf16)
    grad_send = jnp.where(live[:, None], grad_rows, jnp.zeros((), bf16))
    grad_send = grad_send.reshape(local_experts, groups, capacity, width)
    grad_in4 = lax.all_to_all(grad_send, "expert", split_axis=1, concat_axis=1, tiled=True)
    grad_in = flat_rows(grad_in4)
    pre_gate = flat_rows(results[3])
    pre_up = flat_rows(results[4])
    hidden_grad = jnp.einsum("jrd,jfd->jrf", grad_in, w_down, preferred_element_type=f32)
    sig = jax.nn.sigmoid(pre_gate)
    silu_val = pre_gate * sig
    gate_term = (hidden_grad * pre_up * sig * (1.0 + pre_gate * (1.0 - sig))).astype(bf16)
    up_term = (hidden_grad * silu_val).astype(bf16)
    input_grad = (
        jnp.einsum("jrf,jdf->jrd", gate_term, w_gate, preferred_element_type=f32)
        + jnp.einsum("jrf,jdf->jrd", up_term, w_up, preferred_element_type=f32)
    ).astype(bf16)
    input_grad = input_grad.reshape(grad_in4.shape)
    returned = lax.all_to_all(
        input_grad, "expert", split_axis=1, concat_axis=1, tiled=True
    ).reshape(n_experts * capacity, width)
    moe_grad = jnp.sum(returned[dest].reshape(tok_dev, top, width).astype(f32), axis=1)
    chosen_grad = (gate_sens - jnp.sum(gate_sens * gates, axis=1, keepdims=True)) / total
    sel_grad = chosen_grad * chosen * (1.0 - chosen)
    pick = (expert_ids[:, :, None] == ladder[None, None, :]).astype(f32)
    logit_grad = jnp.einsum("tk,tke->te", sel_grad, pick).astype(bf16)
    token_grad = (moe_grad + jnp.dot(logit_grad, router.T, preferred_element_type=f32)).astype(bf16)
    router_grad = lax.psum(
        jnp.dot(tokens.T, logit_grad, preferred_element_type=f32), ("expert", "dp")
    )
    hidden_width = hidden.shape[2]
    arrived4 = results[2]
    columns = (
        lax.all_to_all(arrived4, "dp", split_axis=3, concat_axis=1, tiled=True),
        lax.all_to_all(grad_in4, "dp", split_axis=3, concat_axis=1, tiled=True),
    )
    hid_shape = (local_experts, groups, capacity, hidden_width)
    hiddens = (
        lax.all_gather(gate_term.reshape(hid_shape), "dp", axis=1, tiled=True),
        lax.all_gather(up_term.reshape(hid_shape), "dp", axis=1, tiled=True),
        lax.all_gather(results[1], "dp", axis=1, tiled=True),
    )
    x_cols = flat_rows(columns[0])
    g_cols = flat_rows(columns[1])
    gate_grad = jnp.einsum(
        "jrd,jrf->jdf", x_cols, flat_rows(hiddens[0]), preferred_element_type=f32
    ).astype(bf16)
    up_grad = jnp.einsum(
        "jrd,jrf->jdf", x_cols, flat_rows(hiddens[1]), preferred_element_type=f32
    ).astype(bf16)
    down_grad = jnp.einsum(
        "jrf,jrd->jfd", flat_rows(hiddens[2]), g_cols, preferred_element_type=f32
    ).astype(bf16)
    return (mixed, token_grad, router_grad, gate_grad, up_grad, down_grad)


def solution(mesh):
    placed = (
        P(("expert", "dp"), None),
        P(("expert", "dp"), None),
        P(),
        P("expert", None, None),
        P("expert", None, None),
        P("expert", None, None),
        P(("expert", "dp"), None),
    )
    return jax.shard_map(
        body,
        mesh=mesh,
        in_specs=placed,
        out_specs=(
            P(("expert", "dp"), None),
            P(("expert", "dp"), None),
            P(),
            P("expert", "dp", None),
            P("expert", "dp", None),
            P("expert", None, "dp"),
        ),
        check_vma=False,
    )
```

profile of v0, /device:TPU:0, one launch (start us, length us, event | category | flops | bytes accessed | tf_op | source)
XLA Modules:
  0.0 936.1 jit_solution(13658574191496700082)
XLA Ops:
  8.0 0.9 copy.108
  9.2 4.5 reduce-window.6
  13.8 0.1 copy.111
  14.2 4.3 scatter_custom_fusion
  18.7 6.0 gather_fusion
  24.7 2.7 copy_select_fusion
  27.4 59.9 %all_to_all.50 = bf16[2,8,72,2048]{3,2,0,1:T(8,128)(2,1)S(1)} all-to-all(bf16[2,8,72,2048]{3,2,0,1:T(8,128)(2,1)S(1)} %copy_select_fusion), channel_id=1, replica_groups=mesh['expert'=8,'dp'=4] {'expert'}, dimensions={1} | all-to-all | bytes 9437184 | tf_op jit(solution)/shard_map/all_to_all | solution.py:40
  87.3 0.7 copy.115
  88.1 1.7 copy-done.3
  89.8 3.8 fusion.33
  93.6 5.7 multiply_convert_fusion.2
  99.3 4.1 convolution_convert_fusion
  103.5 2.5 copy.116
  106.0 4.7 all-to-all-start.1
  110.7 0.5 all-gather.8.cloned.1.call-start
  111.2 0.2 all-gather.8.cloned.1.call-update
  111.4 0.1 copy.106
  111.7 0.2 fusion.10
  111.9 7.0 gather_fusion.5
  119.1 5.9 gather_fusion.3
  125.1 40.4 %all-to-all-done.1 = bf16[2,8,72,2048]{3,2,0,1:T(8,128)(2,1)} async-done(((bf16[2,8,72,2048]{3,2,0,1:T(8,128)(2,1)}), bf16[2,8,72,2048]{3,2,0,1:T(8,128)(2,1)}, u32[]{:S(2)}, u32[]{:S(2)}) %all-to-all-start.1) | async-done | bytes 4718624 | tf_op jit(solution)/shard_map/all_to_all | solution.py:53
  165.4 5.2 copy.117
  170.6 11.8 %gather_fusion.1 = bf16[1024,2048]{1,0:T(8,128)(2,1)} fusion(bf16[1152,2048]{1,0:T(8,128)(2,1)} %bitcast.104, s32[1024]{0:T(1024)S(1)} %broadcast_clamp_fusion), kind=kCustom, calls=%fused_computation.1 | custom fusion | bytes 8392704 | tf_op jit(solution)/shard_map/gather | solution.py:56
  182.4 4.9 fusion.2
  187.6 4.6 gather_fusion.2
  192.3 4.4 fusion.1
  196.7 4.6 all-to-all-start.2
  201.3 11.7 %copy.125 = bf16[2,8,72,2048]{2,1,0,3:T(8,128)(2,1)} copy(bf16[2,8,72,2048]{3,2,0,1:T(8,128)(2,1)} %copy-done.3) | data formatting | bytes 9437184 | tf_op jit(solution)/shard_map/all_to_all | solution.py:40
  213.0 43.1 %all-to-all-done.2 = bf16[2,8,72,2048]{3,2,0,1:T(8,128)(2,1)} async-done(((bf16[2,8,72,2048]{3,2,0,1:T(8,128)(2,1)}), bf16[2,8,72,2048]{3,2,0,1:T(8,128)(2,1)}, u32[]{:S(2)}, u32[]{:S(2)}) %all-to-all-start.2) | async-done | bytes 4718624 | tf_op jit(solution)/shard_map/all_to_all | solution.py:62
  256.1 5.6 all-to-all-start.4
  261.7 0.2 all-gather.4.cloned.1.call-start
  261.9 2.9 copy.121
  264.8 0.4 copy-done.11
  265.2 0.9 copy-done.12
  266.1 8.5 multiply_convert_fusion
  274.6 11.3 %fusion.34 = f32[2,576,2048]{2,1,0:T(8,128)} fusion(bf16[2,576,640]{2,1,0:T(8,128)(2,1)} %get-tuple-element.11, bf16[2,2048,640]{2,1,0:T(8,128)(2,1)} %param.10), kind=kOutput, calls=%fused_computation.86 | convolution fusion | flops 3019898880 | bytes 16154624 | tf_op jit(solution)/shard_map/jrf,jdf->jrd/dot_general | solution.py:72
  285.9 8.1 add_convert_fusion
  294.0 2.5 copy.122
  296.5 240.4 %all-to-all-done.4 = bf16[2,8,72,2048]{2,1,0,3:T(8,128)(2,1)} async-done(((bf16[2,8,72,2048]{2,1,0,3:T(8,128)(2,1)}), bf16[2,8,72,2048]{2,1,0,3:T(8,128)(2,1)}, u32[]{:S(2)}, u32[]{:S(2)}) %all-to-all-start.4) | async-done | bytes 4718624 | tf_op jit(solution)/shard_map/all_to_all | solution.py:91
  536.9 5.0 all-to-all-start.3
  541.9 0.7 all-gather.6.cloned.1.call-update
  542.6 11.8 %copy.130 = bf16[2,8,72,2048]{2,1,0,3:T(8,128)(2,1)} copy(bf16[2,8,72,2048]{3,2,0,1:T(8,128)(2,1)} %all-to-all-done.2) | data formatting | bytes 9437184 | tf_op jit(solution)/shard_map/all_to_all | solution.py:62
  554.4 42.3 %all-to-all-done.3 = bf16[2,8,72,2048]{3,2,0,1:T(8,128)(2,1)} async-done(((bf16[2,8,72,2048]{3,2,0,1:T(8,128)(2,1)}), bf16[2,8,72,2048]{3,2,0,1:T(8,128)(2,1)}, u32[]{:S(2)}, u32[]{:S(2)}) %all-to-all-start.3) | async-done | bytes 4718624 | tf_op jit(solution)/shard_map/all_to_all | solution.py:76
  596.7 5.6 all-to-all-start.5
  602.3 0.3 all-reduce.2.cloned.1.call-start
  602.6 0.1 copy.133
  602.8 3.4 fusion.4
  606.2 1.1 copy.154
  607.3 0.1 copy.137
  607.4 0.3 fusion.12
  607.8 0.9 convolution_bitcast_fusion
  608.7 10.7 %copy.142 = bf16[2,8,72,4,512]{4,3,2,1,0:T(4,128)(2,1)} copy(bf16[2,8,72,4,512]{2,1,0,4,3:T(8,128)(2,1)} %bitcast.23) | data formatting | bytes 9437184 | tf_op jit(solution)/shard_map/all_to_all | solution.py:91
  619.4 5.5 copy.127
  624.9 5.3 copy.123
  630.2 11.8 %gather_fusion.4 = bf16[1024,2048]{1,0:T(8,128)(2,1)} fusion(bf16[1152,2048]{1,0:T(8,128)(2,1)} %bitcast.103, s32[1024]{0:T(1024)S(1)} %broadcast_clamp_fusion), kind=kCustom, calls=%fused_computation.4 | custom fusion | bytes 8392704 | tf_op jit(solution)/shard_map/gather | solution.py:79
  641.9 5.0 convert_reduce_fusion
  647.0 1.1 fusion.7
  648.0 185.0 %all-to-all-done.5 = bf16[2,8,72,2048]{2,1,0,3:T(8,128)(2,1)} async-done(((bf16[2,8,72,2048]{2,1,0,3:T(8,128)(2,1)}), bf16[2,8,72,2048]{2,1,0,3:T(8,128)(2,1)}, u32[]{:S(2)}, u32[]{:S(2)}) %all-to-all-start.5) | async-done | bytes 4718624 | tf_op jit(solution)/shard_map/all_to_all | solution.py:92
  833.0 13.3 %copy.131 = bf16[2,8,72,4,512]{4,2,1,3,0:T(8,128)(2,1)} copy(bf16[2,8,72,4,512]{2,1,0,4,3:T(8,128)(2,1)} %bitcast.32) | data formatting | bytes 9437184 | tf_op jit(solution)/shard_map/all_to_all | solution.py:92
  846.4 8.4 convolution_convert_fusion.1
  854.8 9.1 convolution_convert_fusion.3
  863.9 9.2 convolution_convert_fusion.2
  873.1 53.9 %all-reduce.2.cloned.1.call-done = f32[2048,16]{0,1:T(8,128)} async-done(((f32[2048,16]{0,1:T(8,128)}), f32[2048,16]{0,1:T(8,128)}) %all-reduce.2.cloned.1.call-update) | async-done | bytes 131088 | tf_op jit(solution)/shard_map/psum | solution.py:85
  927.0 1.6 copy.156
  (74 shorter events, 1.6 us)
Async XLA Ops:
  8.0 111.1 %copy-start = (bf16[128,2048]{1,0:T(8,128)(2,1)S(1)}, bf16[128,2048]{1,0:T(8,128)(2,1)}, u32[]{:S(2)}) copy-start(bf16[128,2048]{1,0:T(8,128)(2,1)} %param.13) | copy-start | bytes 1572868
  8.0 10.7 %copy-start.2 = (bf16[128,2048]{1,0:T(8,128)(2,1)S(1)}, bf16[128,2048]{1,0:T(8,128)(2,1)}, u32[]{:S(2)}) copy-start(bf16[128,2048]{1,0:T(8,128)(2,1)} %param.7) | copy-start | bytes 1572868
  8.9 15.8 %copy-start.6 = (s32[128,8]{1,0:T(8,128)}, s32[128,8]{1,0:T(8,128)S(1)}, u32[]{:S(2)}) copy-start(s32[128,8]{1,0:T(8,128)S(1)} %copy.108) | copy-start | bytes 12292
  27.4 62.3 %slice-start.2 = ((s8[5242880]{0:T(1024)(128)(4,1)}), s8[4194304]{0:T(1024)(128)(4,1)S(1)}, s32[]{:S(2)}) async-start(s8[5242880]{0:T(1024)(128)(4,1)} %bitcast.133), calls=%async_computation.12 | async-start | bytes 8388608
  87.3 2.4 copy-start.3
  87.3 2.4 slice-start.3
  87.3 6.3 slice-start.4
  89.7 3.9 slice-start.5
  89.7 9.6 %slice-start = ((s8[5242880]{0:T(1024)(128)(4,1)}), s8[4194304]{0:T(1024)(128)(4,1)S(1)}, s32[]{:S(2)}) async-start(s8[5242880]{0:T(1024)(128)(4,1)} %bitcast.131), calls=%async_computation.10 | async-start | bytes 8388608
  93.6 5.7 copy-start.10
  93.6 5.7 slice-start.1
  99.3 4.1 copy-start.4
  106.0 5.5 copy-start.9
  106.0 5.7 copy-start.8
  106.0 59.5 %all-to-all-start.1 = ((bf16[2,8,72,2048]{3,2,0,1:T(8,128)(2,1)}), bf16[2,8,72,2048]{3,2,0,1:T(8,128)(2,1)}, u32[]{:S(2)}, u32[]{:S(2)}) async-start(bf16[2,8,72,2048]{3,2,0,1:T(8,128)(2,1)} %copy.116), calls=%async_computation.1 | async-start | bytes 9437184 | tf_op jit(solution)/shard_map/all_to_all | solution.py:53
  110.7 735.7 %all-gather.8.cloned.1.call-start = ((), (), s32[]{:S(2)}) async-start(), calls=%async_computation.9 | async-start | bytes 7372800 | tf_op jit(solution)/shard_map/all_gather | solution.py:98
  196.7 59.4 %all-to-all-start.2 = ((bf16[2,8,72,2048]{3,2,0,1:T(8,128)(2,1)}), bf16[2,8,72,2048]{3,2,0,1:T(8,128)(2,1)}, u32[]{:S(2)}, u32[]{:S(2)}) async-start(bf16[2,8,72,2048]{3,2,0,1:T(8,128)(2,1)} %fusion.1), calls=%async_computation.2 | async-start | bytes 9437184 | tf_op jit(solution)/shard_map/all_to_all | solution.py:62
  256.1 280.8 %all-to-all-start.4 = ((bf16[2,8,72,2048]{2,1,0,3:T(8,128)(2,1)}), bf16[2,8,72,2048]{2,1,0,3:T(8,128)(2,1)}, u32[]{:S(2)}, u32[]{:S(2)}) async-start(bf16[2,8,72,2048]{2,1,0,3:T(8,128)(2,1)} %copy.125), calls=%async_computation.4 | async-start | bytes 16777216 | tf_op jit(solution)/shard_map/all_to_all | solution.py:91
  261.7 593.1 %all-gather.4.cloned.1.call-start = ((), (), s32[]{:S(2)}) async-start(), calls=%async_computation.7 | async-start | bytes 7372800 | tf_op jit(solution)/shard_map/all_gather | solution.py:96
  261.9 3.3 copy-start.11
  261.9 4.1 copy-start.12
  274.5 11.3 %copy-start.5 = (bf16[2,576,640]{2,1,0:T(8,128)(2,1)}, bf16[2,576,640]{2,1,0:T(8,128)(2,1)S(1)}, u32[]{:S(2)}) copy-start(bf16[2,576,640]{2,1,0:T(8,128)(2,1)S(1)} %get-tuple-element.10) | copy-start | bytes 4423684
  536.9 59.8 %all-to-all-start.3 = ((bf16[2,8,72,2048]{3,2,0,1:T(8,128)(2,1)}), bf16[2,8,72,2048]{3,2,0,1:T(8,128)(2,1)}, u32[]{:S(2)}, u32[]{:S(2)}) async-start(bf16[2,8,72,2048]{3,2,0,1:T(8,128)(2,1)} %copy.122), calls=%async_computation.3 | async-start | bytes 9437184 | tf_op jit(solution)/shard_map/all_to_all | solution.py:76
  541.8 322.1 %all-gather.6.cloned.1.call-start = ((), (), s32[]{:S(2)}) async-start(), calls=%async_computation.8 | async-start | bytes 7372800 | tf_op jit(solution)/shard_map/all_gather | solution.py:97
  596.7 236.3 %all-to-all-start.5 = ((bf16[2,8,72,2048]{2,1,0,3:T(8,128)(2,1)}), bf16[2,8,72,2048]{2,1,0,3:T(8,128)(2,1)}, u32[]{:S(2)}, u32[]{:S(2)}) async-start(bf16[2,8,72,2048]{2,1,0,3:T(8,128)(2,1)} %copy.130), calls=%async_computation.5 | async-start | bytes 16777216 | tf_op jit(solution)/shard_map/all_to_all | solution.py:92
  602.3 5.1 copy-start.7
  602.3 324.6 %all-reduce.2.cloned.1.call-start = ((), (), s32[]{:S(2)}) async-start(), calls=%async_computation.6 | async-start | bytes 262144 | tf_op jit(solution)/shard_map/psum | solution.py:85
  863.9 64.6 %copy-start.1 = (bf16[128,2048]{1,0:T(8,128)(2,1)S(1)}, bf16[128,2048]{1,0:T(8,128)(2,1)}, u32[]{:S(2)}) copy-start(bf16[128,2048]{1,0:T(8,128)(2,1)} %param.13) | copy-start | bytes 1572868
Sparse Core Ops, SparseCore 0:
  113.1 110.4 all-gather.7
  274.7 221.0 all-gather.3
  544.3 178.8 all-gather.5
Sparse Core Ops, SparseCore 1:
  608.9 318.0 all-reduce.1
where the time goes:
time: 946 us; the launch traced here: 936 us
  waiting for transfers between devices  606 us (64%)
  local copies, waits for them, and re-layouts  132 us (14%)
  matrix products  79 us (8%)
  blocking collectives  59.9 us (6%)
  starting transfers between devices  26.6 us (3%)
  other arithmetic  17 us (2%)
  between operations  16.1 us (2%)
    all_to_all x1, waiting for transfers between devices, body(): lax.all_to_all(arrived4, 'dp', split_axis=3, concat_axis=1, tiled=True)  240 us
    all_to_all x1, waiting for transfers between devices, body(): lax.all_to_all(grad_in4, 'dp', split_axis=3, concat_axis=1, tiled=True)  185 us
    all_to_all x1, blocking collectives, body(): lax.all_to_all(send, 'expert', split_axis=1, concat_axis=1, tiled=True)  59.9 us
    psum x1, waiting for transfers between devices, body(): lax.psum(jnp.dot(tokens.T, logit_grad, preferred_element_type=f32), ('exp...  53.9 us
    all_to_all x1, waiting for transfers between devices, body(): lax.all_to_all(grad_send, 'expert', split_axis=1, concat_axis=1, tiled=True)  43.1 us
    all_to_all x1, waiting for transfers between devices, body(): lax.all_to_all(input_grad, 'expert', split_axis=1, concat_axis=1, tiled=T...  42.3 us
    all_to_all x1, waiting for transfers between devices, body(): lax.all_to_all(expert_out, 'expert', split_axis=1, concat_axis=1, tiled=T...  40.4 us
  transfers between devices with their start and end apart: 9, of which 6 were waited for; matrix products, arithmetic and copies ran while one was open for 20% of the time, Pallas kernels for 0%

commit v1 on v0

--- a/solution.py
+++ b/solution.py
@@ -89,7 +89,10 @@
     arrived4 = results[2]
     columns = (
         lax.all_to_all(arrived4, "dp", split_axis=3, concat_axis=1, tiled=True),
-        lax.all_to_all(grad_in4, "dp", split_axis=3, concat_axis=1, tiled=True),
+        jnp.concatenate(
+            lax.all_to_all(jnp.stack(jnp.split(grad_in4, lax.axis_size("dp"), axis=3)), "dp", 0, 0),
+            axis=1,
+        ),
     )
     hid_shape = (local_experts, groups, capacity, hidden_width)
     hiddens = (

time: 946 us -> 866 us (0.915)
  waiting for transfers between devices: 606 us -> 541 us
  local copies, waits for them, and re-layouts: 132 us -> 115 us
    all_to_all x1, waiting for transfers between devices: 185 us -> 107 us  [body(): lax.all_to_all(jnp.stack(jnp.split(grad_in4, lax.axis_size('dp'), axis=3)...]
    all_to_all x1 -> x0, local copies, waits for them, and re-layouts: 13.3 us -> none  [body(): lax.all_to_all(grad_in4, 'dp', split_axis=3, concat_axis=1, tiled=True)]
    all_to_all x2 -> x1, local copies, waits for them, and re-layouts: 14.7 us -> 2.87 us  [body(): lax.all_to_all(grad_send, 'expert', split_axis=1, concat_axis=1, tiled=True)]
where the time goes in v1:
time: 866 us; the launch traced here: 857 us
  waiting for transfers between devices  541 us (62%)
  local copies, waits for them, and re-layouts  115 us (13%)
  matrix products  79.3 us (9%)
  blocking collectives  59.9 us (7%)
  starting transfers between devices  26 us (3%)
  other arithmetic  19.5 us (2%)
  between operations  16.1 us (2%)
    all_to_all x1, waiting for transfers between devices, body(): lax.all_to_all(arrived4, 'dp', split_axis=3, concat_axis=1, tiled=True)  240 us
    all_to_all x1, waiting for transfers between devices, body(): lax.all_to_all(jnp.stack(jnp.split(grad_in4, lax.axis_size('dp'), axis=3)...  107 us
    psum x1, waiting for transfers between devices, body(): lax.psum(jnp.dot(tokens.T, logit_grad, preferred_element_type=f32), ('exp...  60.9 us
    all_to_all x1, blocking collectives, body(): lax.all_to_all(send, 'expert', split_axis=1, concat_axis=1, tiled=True)  59.9 us
    all_to_all x1, waiting for transfers between devices, body(): lax.all_to_all(input_grad, 'expert', split_axis=1, concat_axis=1, tiled=T...  49 us
    all_to_all x1, waiting for transfers between devices, body(): lax.all_to_all(grad_send, 'expert', split_axis=1, concat_axis=1, tiled=True)  43 us
    all_to_all x1, waiting for transfers between devices, body(): lax.all_to_all(expert_out, 'expert', split_axis=1, concat_axis=1, tiled=T...  40.3 us
  transfers between devices with their start and end apart: 9, of which 6 were waited for; matrix products, arithmetic and copies ran while one was open for 20% of the time, Pallas kernels for 0%

profile of v1, /device:TPU:0, one launch (start us, length us, event | category | flops | bytes accessed | tf_op | source)
XLA Modules:
  0.0 856.6 jit_solution(11295224474678694467)
XLA Ops:
  8.0 0.9 copy.106
  9.2 4.5 reduce-window.6
  13.8 0.1 copy.109
  14.2 4.3 scatter_custom_fusion
  18.7 6.0 gather_fusion
  24.7 2.7 copy_select_fusion
  27.4 59.9 %all_to_all.40 = bf16[2,8,72,2048]{3,2,0,1:T(8,128)(2,1)S(1)} all-to-all(bf16[2,8,72,2048]{3,2,0,1:T(8,128)(2,1)S(1)} %copy_select_fusion), channel_id=1, replica_groups=mesh['expert'=8,'dp'=4] {'expert'}, dimensions={1} | all-to-all | bytes 9437184 | tf_op jit(solution)/shard_map/all_to_all | solution.py:40
  87.3 0.7 copy.113
  88.1 1.7 copy-done.3
  89.8 3.8 fusion.33
  93.6 5.7 multiply_convert_fusion.2
  99.3 4.1 convolution_convert_fusion
  103.5 2.5 copy.114
  105.9 4.7 all-to-all-start.1
  110.7 0.6 all-gather.8.cloned.1.call-start
  111.3 0.2 all-gather.8.cloned.1.call-update
  111.7 0.2 fusion.10
  111.9 7.0 gather_fusion.5
  119.1 6.0 gather_fusion.3
  125.1 40.3 %all-to-all-done.1 = bf16[2,8,72,2048]{3,2,0,1:T(8,128)(2,1)} async-done(((bf16[2,8,72,2048]{3,2,0,1:T(8,128)(2,1)}), bf16[2,8,72,2048]{3,2,0,1:T(8,128)(2,1)}, u32[]{:S(2)}, u32[]{:S(2)}) %all-to-all-start.1) | async-done | bytes 4718624 | tf_op jit(solution)/shard_map/all_to_all | solution.py:53
  165.4 5.2 copy.115
  170.6 11.8 %gather_fusion.1 = bf16[1024,2048]{1,0:T(8,128)(2,1)} fusion(bf16[1152,2048]{1,0:T(8,128)(2,1)} %bitcast.110, s32[1024]{0:T(1024)S(1)} %broadcast_clamp_fusion), kind=kCustom, calls=%fused_computation.1 | custom fusion | bytes 8392704 | tf_op jit(solution)/shard_map/gather | solution.py:56
  182.4 4.9 fusion.2
  187.6 4.6 gather_fusion.2
  192.3 4.4 fusion.1
  196.7 4.6 all-to-all-start.2
  201.3 11.7 %copy.123 = bf16[2,8,72,2048]{2,1,0,3:T(8,128)(2,1)} copy(bf16[2,8,72,2048]{3,2,0,1:T(8,128)(2,1)} %copy-done.3) | data formatting | bytes 9437184 | tf_op jit(solution)/shard_map/all_to_all | solution.py:40
  213.0 43.0 %all-to-all-done.2 = bf16[2,8,72,2048]{3,2,0,1:T(8,128)(2,1)} async-done(((bf16[2,8,72,2048]{3,2,0,1:T(8,128)(2,1)}), bf16[2,8,72,2048]{3,2,0,1:T(8,128)(2,1)}, u32[]{:S(2)}, u32[]{:S(2)}) %all-to-all-start.2) | async-done | bytes 4718624 | tf_op jit(solution)/shard_map/all_to_all | solution.py:62
  256.1 5.6 all-to-all-start.4
  261.7 0.2 all-gather.4.cloned.1.call-start
  261.9 2.9 copy.119
  264.8 0.4 copy-done.11
  265.2 0.9 copy-done.12
  266.1 8.5 multiply_convert_fusion
  274.6 11.3 %fusion.34 = f32[2,576,2048]{2,1,0:T(8,128)} fusion(bf16[2,576,640]{2,1,0:T(8,128)(2,1)} %get-tuple-element.11, bf16[2,2048,640]{2,1,0:T(8,128)(2,1)} %param.10), kind=kOutput, calls=%fused_computation.91 | convolution fusion | flops 3019898880 | bytes 16154624 | tf_op jit(solution)/shard_map/jrf,jdf->jrd/dot_general | solution.py:72
  285.9 8.1 add_convert_fusion
  294.0 2.5 copy.120
  296.5 240.4 %all-to-all-done.4 = bf16[2,8,72,2048]{2,1,0,3:T(8,128)(2,1)} async-done(((bf16[2,8,72,2048]{2,1,0,3:T(8,128)(2,1)}), bf16[2,8,72,2048]{2,1,0,3:T(8,128)(2,1)}, u32[]{:S(2)}, u32[]{:S(2)}) %all-to-all-start.4) | async-done | bytes 4718624 | tf_op jit(solution)/shard_map/all_to_all | solution.py:91
  536.9 5.0 all-to-all-start.3
  541.9 0.7 all-gather.6.cloned.1.call-update
  542.6 2.7 slice_bitcast_fusion.3
  545.3 2.5 pad_maximum_fusion
  547.7 49.0 %all-to-all-done.3 = bf16[2,8,72,2048]{3,2,0,1:T(8,128)(2,1)} async-done(((bf16[2,8,72,2048]{3,2,0,1:T(8,128)(2,1)}), bf16[2,8,72,2048]{3,2,0,1:T(8,128)(2,1)}, u32[]{:S(2)}, u32[]{:S(2)}) %all-to-all-start.3) | async-done | bytes 4718624 | tf_op jit(solution)/shard_map/all_to_all | solution.py:76
  596.7 5.0 all-to-all-start.5
  601.7 0.3 all-reduce.2.cloned.1.call-start
  601.9 0.1 copy.130
  602.1 3.4 fusion.4
  605.5 1.1 copy.151
  606.6 0.1 copy.134
  606.8 0.3 fusion.12
  607.1 0.9 convolution_bitcast_fusion
  608.0 10.7 %copy.139 = bf16[2,8,72,4,512]{4,3,2,1,0:T(4,128)(2,1)} copy(bf16[2,8,72,4,512]{2,1,0,4,3:T(8,128)(2,1)} %bitcast.23) | data formatting | bytes 9437184 | tf_op jit(solution)/shard_map/all_to_all | solution.py:91
  618.7 5.6 copy.125
  624.3 5.3 copy.121
  629.6 12.0 %gather_fusion.4 = bf16[1024,2048]{1,0:T(8,128)(2,1)} fusion(bf16[1152,2048]{1,0:T(8,128)(2,1)} %bitcast.109, s32[1024]{0:T(1024)S(1)} %broadcast_clamp_fusion), kind=kCustom, calls=%fused_computation.4 | custom fusion | bytes 8392704 | tf_op jit(solution)/shard_map/gather | solution.py:79
  641.6 5.0 convert_reduce_fusion
  646.6 1.1 fusion.7
  647.7 106.7 %all-to-all-done.5 = bf16[4,2,8,72,512]{4,3,1,2,0:T(8,128)(2,1)} async-done(((bf16[4,2,8,72,512]{4,3,1,2,0:T(8,128)(2,1)}), bf16[4,2,8,72,512]{4,3,1,2,0:T(8,128)(2,1)}, u32[]{:S(2)}, u32[]{:S(2)}) %all-to-all-start.5) | async-done | bytes 4718624 | tf_op jit(solution)/shard_map/all_to_all | solution.py:93
  754.4 5.0 copy.128
  759.5 8.4 convolution_convert_fusion.1
  767.8 9.1 %convolution_convert_fusion.3 = bf16[2,512,640]{2,1,0:T(8,128)(2,1)} fusion(bf16[2,2304,512]{2,1,0:T(8,128)(2,1)} %bitcast.114, bf16[2,2304,640]{2,1,0:T(8,128)(2,1)} %bitcast.135), kind=kOutput, calls=%fused_computation.29 | convolution fusion | flops 3020554240 | bytes 11927552 | tf_op jit(solution)/shard_map/jrd,jrf->jdf/dot_general | solution.py:105
  777.0 9.5 %convolution_convert_fusion.2 = bf16[2,512,640]{2,1,0:T(8,128)(2,1)} fusion(bf16[2,2304,512]{2,1,0:T(8,128)(2,1)} %bitcast.115, bf16[2,2304,640]{2,1,0:T(8,128)(2,1)} %bitcast.136), kind=kOutput, calls=%fused_computation.28 | convolution fusion | flops 3020554240 | bytes 11927552 | tf_op jit(solution)/shard_map/jrd,jrf->jdf/dot_general | solution.py:108
  786.4 60.9 %all-reduce.2.cloned.1.call-done = f32[2048,16]{0,1:T(8,128)} async-done(((f32[2048,16]{0,1:T(8,128)}), f32[2048,16]{0,1:T(8,128)}) %all-reduce.2.cloned.1.call-update) | async-done | bytes 131088 | tf_op jit(solution)/shard_map/psum | solution.py:85
  847.4 1.6 copy.153
  (75 shorter events, 1.7 us)
Async XLA Ops:
  8.0 111.1 %copy-start = (bf16[128,2048]{1,0:T(8,128)(2,1)S(1)}, bf16[128,2048]{1,0:T(8,128)(2,1)}, u32[]{:S(2)}) copy-start(bf16[128,2048]{1,0:T(8,128)(2,1)} %param.13) | copy-start | bytes 1572868
  8.0 10.7 %copy-start.2 = (bf16[128,2048]{1,0:T(8,128)(2,1)S(1)}, bf16[128,2048]{1,0:T(8,128)(2,1)}, u32[]{:S(2)}) copy-start(bf16[128,2048]{1,0:T(8,128)(2,1)} %param.7) | copy-start | bytes 1572868
  8.9 15.8 %copy-start.6 = (s32[128,8]{1,0:T(8,128)}, s32[128,8]{1,0:T(8,128)S(1)}, u32[]{:S(2)}) copy-start(s32[128,8]{1,0:T(8,128)S(1)} %copy.106) | copy-start | bytes 12292
  27.4 62.3 %slice-start.2 = ((s8[5242880]{0:T(1024)(128)(4,1)}), s8[4194304]{0:T(1024)(128)(4,1)S(1)}, s32[]{:S(2)}) async-start(s8[5242880]{0:T(1024)(128)(4,1)} %bitcast.139), calls=%async_computation.12 | async-start | bytes 8388608
  87.3 2.4 copy-start.3
  87.3 2.4 slice-start.3
  87.3 6.3 slice-start.4
  89.7 3.9 slice-start.5
  89.8 9.6 %slice-start = ((s8[5242880]{0:T(1024)(128)(4,1)}), s8[4194304]{0:T(1024)(128)(4,1)S(1)}, s32[]{:S(2)}) async-start(s8[5242880]{0:T(1024)(128)(4,1)} %bitcast.137), calls=%async_computation.10 | async-start | bytes 8388608
  93.6 5.7 copy-start.10
  93.6 5.7 slice-start.1
  99.3 4.1 copy-start.4
  105.9 5.5 copy-start.9
  105.9 5.7 copy-start.8
  105.9 59.5 %all-to-all-start.1 = ((bf16[2,8,72,2048]{3,2,0,1:T(8,128)(2,1)}), bf16[2,8,72,2048]{3,2,0,1:T(8,128)(2,1)}, u32[]{:S(2)}, u32[]{:S(2)}) async-start(bf16[2,8,72,2048]{3,2,0,1:T(8,128)(2,1)} %copy.114), calls=%async_computation.1 | async-start | bytes 9437184 | tf_op jit(solution)/shard_map/all_to_all | solution.py:53
  110.7 648.8 %all-gather.8.cloned.1.call-start = ((), (), s32[]{:S(2)}) async-start(), calls=%async_computation.9 | async-start | bytes 7372800 | tf_op jit(solution)/shard_map/all_gather | solution.py:101
  196.7 59.4 %all-to-all-start.2 = ((bf16[2,8,72,2048]{3,2,0,1:T(8,128)(2,1)}), bf16[2,8,72,2048]{3,2,0,1:T(8,128)(2,1)}, u32[]{:S(2)}, u32[]{:S(2)}) async-start(bf16[2,8,72,2048]{3,2,0,1:T(8,128)(2,1)} %fusion.1), calls=%async_computation.2 | async-start | bytes 9437184 | tf_op jit(solution)/shard_map/all_to_all | solution.py:62
  256.1 280.8 %all-to-all-start.4 = ((bf16[2,8,72,2048]{2,1,0,3:T(8,128)(2,1)}), bf16[2,8,72,2048]{2,1,0,3:T(8,128)(2,1)}, u32[]{:S(2)}, u32[]{:S(2)}) async-start(bf16[2,8,72,2048]{2,1,0,3:T(8,128)(2,1)} %copy.123), calls=%async_computation.4 | async-start | bytes 16777216 | tf_op jit(solution)/shard_map/all_to_all | solution.py:91
  261.7 506.1 %all-gather.4.cloned.1.call-start = ((), (), s32[]{:S(2)}) async-start(), calls=%async_computation.7 | async-start | bytes 7372800 | tf_op jit(solution)/shard_map/all_gather | solution.py:99
  261.9 3.3 copy-start.11
  261.9 4.1 copy-start.12
  274.5 11.3 %copy-start.5 = (bf16[2,576,640]{2,1,0:T(8,128)(2,1)}, bf16[2,576,640]{2,1,0:T(8,128)(2,1)S(1)}, u32[]{:S(2)}) copy-start(bf16[2,576,640]{2,1,0:T(8,128)(2,1)S(1)} %get-tuple-element.10) | copy-start | bytes 4423684
  536.9 59.8 %all-to-all-start.3 = ((bf16[2,8,72,2048]{3,2,0,1:T(8,128)(2,1)}), bf16[2,8,72,2048]{3,2,0,1:T(8,128)(2,1)}, u32[]{:S(2)}, u32[]{:S(2)}) async-start(bf16[2,8,72,2048]{3,2,0,1:T(8,128)(2,1)} %copy.120), calls=%async_computation.3 | async-start | bytes 9437184 | tf_op jit(solution)/shard_map/all_to_all | solution.py:76
  541.9 235.1 %all-gather.6.cloned.1.call-start = ((), (), s32[]{:S(2)}) async-start(), calls=%async_computation.8 | async-start | bytes 7372800 | tf_op jit(solution)/shard_map/all_gather | solution.py:100
  596.7 157.7 %all-to-all-start.5 = ((bf16[4,2,8,72,512]{4,3,1,2,0:T(8,128)(2,1)}), bf16[4,2,8,72,512]{4,3,1,2,0:T(8,128)(2,1)}, u32[]{:S(2)}, u32[]{:S(2)}) async-start(bf16[4,2,8,72,512]{4,3,1,2,0:T(8,128)(2,1)} %pad_maximum_fusion), calls=%async_computation.5 | async-start | bytes 9437184 | tf_op jit(solution)/shard_map/all_to_all | solution.py:93
  601.7 5.1 copy-start.7
  601.7 245.7 %all-reduce.2.cloned.1.call-start = ((), (), s32[]{:S(2)}) async-start(), calls=%async_computation.6 | async-start | bytes 262144 | tf_op jit(solution)/shard_map/psum | solution.py:85
  777.0 72.0 %copy-start.1 = (bf16[128,2048]{1,0:T(8,128)(2,1)S(1)}, bf16[128,2048]{1,0:T(8,128)(2,1)}, u32[]{:S(2)}) copy-start(bf16[128,2048]{1,0:T(8,128)(2,1)} %param.13) | copy-start | bytes 1572868
Sparse Core Ops, SparseCore 0:
  113.1 110.4 all-gather.7
  274.7 221.0 all-gather.3
  544.3 184.8 all-gather.5
Sparse Core Ops, SparseCore 1:
  608.3 239.0 all-reduce.1
